TPU v7x, 512 devices: a whole 4x8x8 slice. The times are simulated.
512 devices in a mesh: subj: 32 (over z, y_lo), slab: 16 (over y_hi, x, core).
Axes of the slice: x: 4, y: 8 (y_hi: 2, y_lo: 4; y = y_hi * 4 + y_lo), z: 8, core: 2. Of those that a mesh axis runs over, the one named last changes fastest.
Arguments:
- data_rhs: float32 [32, 16, 64, 1536], P('subj', None, 'slab'), may hold values from -12 to 12
- inv_var: float32 [32, 64, 1536], P('subj', 'slab'), may hold values from 0.01 to 0.3
- design: float32 [32, 16], P('subj'), may hold values from 0.5 to 4
- keep_mask: int32 [32, 64, 1536], P('subj', 'slab'), may hold values 0 or 1
- brain_mask: int32 [64, 1536], P('slab'), may hold values 0 or 1
- tissue: int32 [64, 1536], P('slab'), may hold values from 0 to 2
- kappa_sq: float32 [3, 16], replicated, may hold values from 0.005 to 0.5
- prior_scale: float32 [16], replicated, may hold values from 0.5 to 2
- mean_field: float32 [16, 64, 1536], P(None, 'slab', 'subj'), may hold values from -6 to 6
- pop_noise: float32 [16, 64, 1536], P(None, 'slab', 'subj'), may hold values from -6 to 6
Outputs:
- subject_fields: float32 [32, 16, 64, 1536], P('subj', None, 'slab')
- new_mean: float32 [16, 64, 1536], P(None, 'slab', 'subj')
All inputs are finite; a program needn't handle non-finite values. No bound on the sum of `keep_mask` or of `brain_mask` on one device may be relied on, other than what follows from the above.
Results may differ from a plain program's by a relative error of at most 0.00016.
Values sent between devices are 32-bit elements; how exact they have to be, the bound alone decides.
A program may use at most 64 MiB of HBM per device.

v0:
```python
import math
import jax
import jax.numpy as jnp
from jax import lax
from jax.sharding import PartitionSpec as P

CLASSES = 3
ITERS = 8
CX = 64
MEAN_PRECISION = 1.0


def padded_2(cells, sides, width):
    for axis, dim in sides:
        count = lax.axis_size(axis)
        ends = count - 1
        head = lax.slice_in_dim(cells, 0, width, axis=dim)
        tail = lax.slice_in_dim(cells, cells.shape[dim] - width, cells.shape[dim], axis=dim)
        cells = jnp.concatenate(
            [
                lax.ppermute(tail, axis, [(i, (i + 1) % count) for i in range(ends)]),
                cells,
                lax.ppermute(head, axis, [((i + 1) % count, i) for i in range(ends)]),
            ],
            axis=dim,
        )
    return cells


def plane_beside(center):
    cells = center.shape[-1]
    column = lax.iota(jnp.int32, cells) % CX
    zeros_one = jnp.zeros(center.shape[:-1] + (1,), jnp.float32)
    zeros_row = jnp.zeros(center.shape[:-1] + (CX,), jnp.float32)
    from_left = jnp.where(column > 0, jnp.concatenate([zeros_one, center[..., :-1]], axis=-1), 0.0)
    from_right = jnp.where(
        column < CX - 1, jnp.concatenate([center[..., 1:], zeros_one], axis=-1), 0.0
    )
    from_below = jnp.concatenate([zeros_row, center[..., :-CX]], axis=-1)
    from_above = jnp.concatenate([center[..., CX:], zeros_row], axis=-1)
    return from_left + from_right + from_below + from_above


def beside_of(padded):
    center = padded[:, :, 1:-1]
    return padded[:, :, 2:] + padded[:, :, :-2] + plane_beside(center)


def local(
    data_rhs,
    inv_var,
    design,
    keep_mask,
    brain_mask,
    tissue,
    kappa_sq,
    prior_scale,
    mean_field,
    pop_noise,
):
    in_brain = brain_mask.astype(jnp.float32)
    kappa_field = jnp.zeros((prior_scale.shape[0],) + tissue.shape, jnp.float32)
    for label in range(CLASSES):
        kappa_field = (
            kappa_field
            + jnp.where(tissue == label, 1.0, 0.0)[None] * kappa_sq[label][:, None, None]
        )
    scale_col = prior_scale[:, None, None]
    shifted = 6.0 + kappa_field
    whole_mean = lax.all_gather(mean_field, "subj", axis=2, tiled=True)
    padded_mean = padded_2(whole_mean[None], (("slab", 2),), 1)
    prior_mean = scale_col * (shifted * padded_mean[:, :, 1:-1] - beside_of(padded_mean))
    voxel_factor = inv_var * in_brain * keep_mask.astype(jnp.float32)
    diagonal = design[:, :, None, None] * voxel_factor[:, None] + scale_col * shifted
    right_side = data_rhs + prior_mean

    def inner(left, right):
        return jnp.sum(left * right, axis=(2, 3))

    solution = jnp.zeros_like(right_side)
    residual = right_side

    def residual_norm(current):
        local_norm = inner(current, current)
        return lax.psum(local_norm, "slab")

    direction = right_side
    norm_now = residual_norm(residual)
    for iteration in range(ITERS):
        applied = diagonal * direction - scale_col * beside_of(
            padded_2(direction, (("slab", 2),), 1)
        )
        local_curv = inner(direction, applied)
        curv_sum = lax.psum(local_curv, "slab")
        step_size = norm_now / curv_sum
        solution = solution + step_size[:, :, None, None] * direction
        if iteration + 1 < ITERS:
            residual = residual - step_size[:, :, None, None] * applied
            norm_next = residual_norm(residual)
            direction = residual + (norm_next / norm_now)[:, :, None, None] * direction
            norm_now = norm_next
    subject_total = jnp.sum(solution, axis=0)
    summed = lax.psum_scatter(subject_total, "subj", scatter_dimension=2, tiled=True)
    subjects = design.shape[0] * lax.axis_size("subj")
    divisor = subjects + MEAN_PRECISION
    new_mean = summed / divisor + pop_noise / math.sqrt(divisor)
    return (solution, new_mean)


def solution(mesh):
    in_specs = (
        P("subj", None, "slab", None),
        P("subj", "slab", None),
        P("subj", None),
        P("subj", "slab", None),
        P("slab", None),
        P("slab", None),
        P(),
        P(),
        P(None, "slab", "subj"),
        P(None, "slab", "subj"),
    )
    out_specs = (P("subj", None, "slab", None), P(None, "slab", "subj"))
    return jax.shard_map(local, mesh=mesh, in_specs=in_specs, out_specs=out_specs, check_vma=False)
```

profile of v0, /device:TPU:4, one launch (start us, length us, event | category | flops | bytes accessed | tf_op | source)
XLA Modules:
  0.0 1116.8 jit_solution(7056748842792953106)
XLA Ops:
  8.1 126.5 %all_gather.3 = f32[16,4,1536]{0,1,2:T(4,128)} all-gather(f32[16,4,48]{0,1,2:T(4,128)S(1)} %copy.79), channel_id=1, replica_groups=mesh['subj'=32,'slab'=16] {'subj'}, dimensions={2}, use_global_device_ids=true | all-gather | bytes 405504 | tf_op jit(solution)/shard_map/all_gather | solution.py:70
  134.6 3.1 copy.80
  151.8 3.7 collective-permute-done.3
  156.1 40.7 %all-reduce.36 = (f32[1,16]{1,0:T(1,128)S(1)}, f32[1,16]{1,0:T(1,128)S(1)}) all-reduce(f32[1,16]{1,0:T(1,128)S(1)} %bitcast.85, f32[1,16]{1,0:T(1,128)S(1)} %bitcast.84), channel_id=1, replica_groups=mesh['subj'=32,'slab'=16] {'slab'}, use_global_device_ids=true, to_apply=%region_1.2 | all-reduce | flops 32 | bytes 256 | tf_op jit(solution)/shard_map/psum | solution.py:85
  197.0 42.8 %psum.114 = f32[1,16]{1,0:T(1,128)S(1)} all-reduce(f32[1,16]{1,0:T(1,128)S(1)} %bitcast.90), channel_id=1, replica_groups=mesh['subj'=32,'slab'=16] {'slab'}, use_global_device_ids=true, to_apply=%region_5.6 | all-reduce | flops 16 | bytes 128 | tf_op jit(solution)/shard_map/psum | solution.py:85
  242.2 2.5 collective-permute-start.5
  244.9 3.3 collective-permute-done.5
  249.3 48.8 %psum.115 = f32[1,16]{1,0:T(1,128)S(1)} all-reduce(f32[1,16]{1,0:T(1,128)S(1)} %bitcast.92), channel_id=1, replica_groups=mesh['subj'=32,'slab'=16] {'slab'}, use_global_device_ids=true, to_apply=%region_7.8 | all-reduce | flops 16 | bytes 128 | tf_op jit(solution)/shard_map/psum | solution.py:94
  299.7 42.8 %psum.116 = f32[1,16]{1,0:T(1,128)S(1)} all-reduce(f32[1,16]{1,0:T(1,128)S(1)} %bitcast.82), channel_id=1, replica_groups=mesh['subj'=32,'slab'=16] {'slab'}, use_global_device_ids=true, to_apply=%region_9.10 | all-reduce | flops 16 | bytes 128 | tf_op jit(solution)/shard_map/psum | solution.py:85
  345.4 2.5 collective-permute-start.7
  348.0 3.3 collective-permute-done.7
  352.5 48.8 %psum.117 = f32[1,16]{1,0:T(1,128)S(1)} all-reduce(f32[1,16]{1,0:T(1,128)S(1)} %bitcast.93), channel_id=1, replica_groups=mesh['subj'=32,'slab'=16] {'slab'}, use_global_device_ids=true, to_apply=%region_11.12 | all-reduce | flops 16 | bytes 128 | tf_op jit(solution)/shard_map/psum | solution.py:94
  402.2 42.8 %psum.118 = f32[1,16]{1,0:T(1,128)S(1)} all-reduce(f32[1,16]{1,0:T(1,128)S(1)} %bitcast.86), channel_id=1, replica_groups=mesh['subj'=32,'slab'=16] {'slab'}, use_global_device_ids=true, to_apply=%region_13.14 | all-reduce | flops 16 | bytes 128 | tf_op jit(solution)/shard_map/psum | solution.py:85
  447.9 2.5 collective-permute-start.9
  450.6 3.3 collective-permute-done.9
  455.0 48.8 %psum.119 = f32[1,16]{1,0:T(1,128)S(1)} all-reduce(f32[1,16]{1,0:T(1,128)S(1)} %bitcast.94), channel_id=1, replica_groups=mesh['subj'=32,'slab'=16] {'slab'}, use_global_device_ids=true, to_apply=%region_15.16 | all-reduce | flops 16 | bytes 128 | tf_op jit(solution)/shard_map/psum | solution.py:94
  504.7 42.8 %psum.120 = f32[1,16]{1,0:T(1,128)S(1)} all-reduce(f32[1,16]{1,0:T(1,128)S(1)} %bitcast.87), channel_id=1, replica_groups=mesh['subj'=32,'slab'=16] {'slab'}, use_global_device_ids=true, to_apply=%region_17.18 | all-reduce | flops 16 | bytes 128 | tf_op jit(solution)/shard_map/psum | solution.py:85
  553.1 3.3 collective-permute-done.11
  557.5 48.8 %psum.121 = f32[1,16]{1,0:T(1,128)S(1)} all-reduce(f32[1,16]{1,0:T(1,128)S(1)} %bitcast.95), channel_id=1, replica_groups=mesh['subj'=32,'slab'=16] {'slab'}, use_global_device_ids=true, to_apply=%region_19.20 | all-reduce | flops 16 | bytes 128 | tf_op jit(solution)/shard_map/psum | solution.py:94
  607.3 42.8 %psum.122 = f32[1,16]{1,0:T(1,128)S(1)} all-reduce(f32[1,16]{1,0:T(1,128)S(1)} %bitcast.88), channel_id=1, replica_groups=mesh['subj'=32,'slab'=16] {'slab'}, use_global_device_ids=true, to_apply=%region_21.22 | all-reduce | flops 16 | bytes 128 | tf_op jit(solution)/shard_map/psum | solution.py:85
  655.6 3.3 collective-permute-done.13
  660.1 48.8 %psum.123 = f32[1,16]{1,0:T(1,128)S(1)} all-reduce(f32[1,16]{1,0:T(1,128)S(1)} %bitcast.96), channel_id=1, replica_groups=mesh['subj'=32,'slab'=16] {'slab'}, use_global_device_ids=true, to_apply=%region_23.24 | all-reduce | flops 16 | bytes 128 | tf_op jit(solution)/shard_map/psum | solution.py:94
  710.4 42.9 %psum.124 = f32[1,16]{1,0:T(1,128)S(1)} all-reduce(f32[1,16]{1,0:T(1,128)} %bitcast.89), channel_id=1, replica_groups=mesh['subj'=32,'slab'=16] {'slab'}, use_global_device_ids=true, to_apply=%region_25.26 | all-reduce | flops 16 | bytes 128 | tf_op jit(solution)/shard_map/psum | solution.py:85
  756.2 2.5 collective-permute-start.15
  758.8 3.3 collective-permute-done.15
  764.0 49.5 %psum.125 = f32[1,16]{1,0:T(1,128)} all-reduce(f32[1,16]{1,0:T(1,128)} %bitcast.97), channel_id=1, replica_groups=mesh['subj'=32,'slab'=16] {'slab'}, use_global_device_ids=true, to_apply=%region_27.28 | all-reduce | flops 16 | bytes 128 | tf_op jit(solution)/shard_map/psum | solution.py:94
  815.4 43.4 %psum.126 = f32[1,16]{1,0:T(1,128)} all-reduce(f32[1,16]{1,0:T(1,128)} %bitcast.91), channel_id=1, replica_groups=mesh['subj'=32,'slab'=16] {'slab'}, use_global_device_ids=true, to_apply=%region_29.30 | all-reduce | flops 16 | bytes 128 | tf_op jit(solution)/shard_map/psum | solution.py:85
  865.4 3.3 collective-permute-done.17
  870.5 49.1 %psum.127 = f32[1,16]{1,0:T(1,128)S(1)} all-reduce(f32[1,16]{1,0:T(1,128)} %bitcast.83), channel_id=1, replica_groups=mesh['subj'=32,'slab'=16] {'slab'}, use_global_device_ids=true, to_apply=%region_31.32 | all-reduce | flops 16 | bytes 128 | tf_op jit(solution)/shard_map/psum | solution.py:94
  921.3 8.3 copy.85
  929.6 9.8 reshape.112
  940.5 167.6 %reduce-scatter.4.cloned.1.call-done = f32[48,64]{1,0:T(8,128)} async-done(((f32[1536,64]{1,0:T(8,128)}), f32[48,64]{1,0:T(8,128)}) %reduce-scatter.4.cloned.1.call-update) | async-done | bytes 12304
  (145 shorter events, 66.8 us)
Async XLA Ops:
  7.2 148.4 %copy-start.6 = (f32[16]{0:T(128)S(1)}, f32[16]{0:T(128)}, u32[]{:S(2)}) copy-start(f32[16]{0:T(128)} %param.17) | copy-start | bytes 196
  7.2 148.4 %copy-start.8 = (f32[1,16]{1,0:T(1,128)S(1)}, f32[1,16]{1,0:T(1,128)}, u32[]{:S(2)}) copy-start(f32[1,16]{1,0:T(1,128)} %param.12) | copy-start | bytes 196
  7.2 1100.9 %reduce-scatter.4.cloned.1.call-start = ((), (), s32[]{:S(2)}) async-start(), calls=%async_computation.1 | async-start | bytes 811008
  137.7 7.1 collective-permute-start
  139.6 5.9 collective-permute-start.1
  143.2 96.9 %copy-start.5 = (f32[16]{0:T(128)}, f32[16]{0:T(128)S(1)}, u32[]{:S(2)}) copy-start(f32[16]{0:T(128)S(1)} %get-tuple-element.94) | copy-start | bytes 196
  144.0 514.9 %copy-start.1 = (f32[4,1536]{1,0:T(4,128)}, f32[4,1536]{1,0:T(4,128)S(1)}, u32[]{:S(2)}) copy-start(f32[4,1536]{1,0:T(4,128)S(1)} %get-tuple-element.89) | copy-start | bytes 73732
  144.0 514.9 %copy-start.2 = (f32[4,1536]{1,0:T(4,128)}, f32[4,1536]{1,0:T(4,128)S(1)}, u32[]{:S(2)}) copy-start(f32[4,1536]{1,0:T(4,128)S(1)} %get-tuple-element.90) | copy-start | bytes 73732
  144.0 514.9 %copy-start.3 = (f32[4,1536]{1,0:T(4,128)}, f32[4,1536]{1,0:T(4,128)S(1)}, u32[]{:S(2)}) copy-start(f32[4,1536]{1,0:T(4,128)S(1)} %get-tuple-element.91) | copy-start | bytes 73732
  144.8 514.1 %copy-start.4 = (f32[4,1536]{1,0:T(4,128)}, f32[4,1536]{1,0:T(4,128)S(1)}, u32[]{:S(2)}) copy-start(f32[4,1536]{1,0:T(4,128)S(1)} %fusion.40) | copy-start | bytes 73732
  147.2 4.6 collective-permute-start.2
  149.6 5.9 collective-permute-start.3
  240.3 4.6 collective-permute-start.4
  242.2 5.9 collective-permute-start.5
  298.8 44.6 %copy-start.11 = (f32[16]{0:T(128)}, f32[16]{0:T(128)S(1)}, u32[]{:S(2)}) copy-start(f32[16]{0:T(128)S(1)} %divide_bitcast_fusion.12) | copy-start | bytes 196
  343.4 4.6 collective-permute-start.6
  345.4 5.9 collective-permute-start.7
  401.9 44.0 %copy-start.12 = (f32[16]{0:T(128)}, f32[16]{0:T(128)S(1)}, u32[]{:S(2)}) copy-start(f32[16]{0:T(128)S(1)} %divide_bitcast_fusion.10) | copy-start | bytes 196
  446.0 4.6 collective-permute-start.8
  447.9 5.9 collective-permute-start.9
  504.5 44.0 %copy-start.13 = (f32[16]{0:T(128)}, f32[16]{0:T(128)S(1)}, u32[]{:S(2)}) copy-start(f32[16]{0:T(128)S(1)} %divide_bitcast_fusion.8) | copy-start | bytes 196
  548.5 4.6 collective-permute-start.10
  550.4 5.9 collective-permute-start.11
  607.0 51.9 %copy-start.14 = (f32[16]{0:T(128)}, f32[16]{0:T(128)S(1)}, u32[]{:S(2)}) copy-start(f32[16]{0:T(128)S(1)} %divide_bitcast_fusion.6) | copy-start | bytes 196
  651.0 4.6 collective-permute-start.12
  653.0 5.9 collective-permute-start.13
  754.2 4.6 collective-permute-start.14
  756.2 5.9 collective-permute-start.15
  763.9 94.9 %copy-start = (f32[1,16,4,1536]{3,1,2,0:T(8,128)}, f32[1,16,4,1536]{3,1,2,0:T(8,128)S(1)}, u32[]{:S(2)}) copy-start(f32[1,16,4,1536]{3,1,2,0:T(8,128)S(1)} %get-tuple-element.13) | copy-start | bytes 1179652
  860.8 4.6 collective-permute-start.16
  862.7 5.9 collective-permute-start.17
  921.3 188.0 %copy-start.7 = (f32[16,4,48]{2,1,0:T(4,128)S(1)}, f32[16,4,48]{2,1,0:T(4,128)}, u32[]{:S(2)}) copy-start(f32[16,4,48]{2,1,0:T(4,128)} %param.19) | copy-start | bytes 36868
  (9 other events, 57.7 us)
Sparse Core Ops, SparseCore 0:
  939.6 168.4 reduce-scatter.3
where the time goes:
time: 1120 us
  blocking collectives  810 us (72%)
  waiting for transfers between devices  195 us (17%)
  starting transfers between devices  39.5 us (4%)
  local copies, waits for them, and re-layouts  29 us (3%)
  other arithmetic  28.6 us (3%)
  between operations  14.6 us (1%)
    psum x7, blocking collectives, local(): curv_sum = lax.psum(local_curv, 'slab')  343 us
    psum x8, blocking collectives, residual_norm(): return lax.psum(local_norm, 'slab')  341 us
    unnamed x2, waiting for transfers between devices  168 us
    all_gather x1, blocking collectives, local(): whole_mean = lax.all_gather(mean_field, 'subj', axis=2, tiled=True)  127 us
    ppermute x9, waiting for transfers between devices, padded_2(): lax.ppermute(tail, axis, [(i, (i + 1) % count) for i in range(ends)])  27.4 us
  transfers between devices with their start and end apart: 19, of which 11 were waited for; matrix products, arithmetic and copies ran while one was open for 0% of the time, Pallas kernels for 0%

commit v1 on v0

--- a/solution.py
+++ b/solution.py
@@ -67,7 +67,9 @@
         )
     scale_col = prior_scale[:, None, None]
     shifted = 6.0 + kappa_field
-    whole_mean = lax.all_gather(mean_field, "subj", axis=2, tiled=True)
+    whole_mean = jnp.concatenate(
+        lax.all_to_all(jnp.stack([mean_field] * lax.axis_size("subj")), "subj", 0, 0), axis=2
+    )
     padded_mean = padded_2(whole_mean[None], (("slab", 2),), 1)
     prior_mean = scale_col * (shifted * padded_mean[:, :, 1:-1] - beside_of(padded_mean))
     voxel_factor = inv_var * in_brain * keep_mask.astype(jnp.float32)

time: 1120 us -> 1030 us (0.920)
  the two profiles are of different devices: /device:TPU:4 before, /device:TPU:6 now
where the time goes in v1:
time: 1030 us
  blocking collectives  694 us (67%)
  waiting for transfers between devices  202 us (20%)
  starting transfers between devices  56.3 us (5%)
  local copies, waits for them, and re-layouts  31 us (3%)
  other arithmetic  29.1 us (3%)
  between operations  14.6 us (1%)
    psum x8, blocking collectives, residual_norm(): return lax.psum(local_norm, 'slab')  352 us
    psum x7, blocking collectives, local(): curv_sum = lax.psum(local_curv, 'slab')  342 us
    unnamed x2, waiting for transfers between devices  163 us
    ppermute x9, waiting for transfers between devices, padded_2(): lax.ppermute(tail, axis, [(i, (i + 1) % count) for i in range(ends)])  26.8 us
    ppermute x9, starting transfers between devices, padded_2(): lax.ppermute(tail, axis, [(i, (i + 1) % count) for i in range(ends)])  25.2 us
    unnamed x53, local copies, waits for them, and re-layouts  24.2 us
  transfers between devices with their start and end apart: 20, of which 11 were waited for; matrix products, arithmetic and copies ran while one was open for 0% of the time, Pallas kernels for 0%

profile of v1, /device:TPU:6, one launch (start us, length us, event | category | flops | bytes accessed | tf_op | source)
XLA Modules:
  0.0 1027.6 jit_solution(11373890814411751842)
XLA Ops:
  10.2 13.7 %all-to-all-start = ((f32[32,1,3072]{2,1,0:T(1,128)}), f32[32,1,3072]{2,1,0:T(1,128)S(1)}, u32[]{:S(2)}, u32[]{:S(2)}) async-start(f32[32,1,3072]{2,1,0:T(1,128)} %reshape.131), calls=%async_computation | async-start | bytes 786432 | tf_op jit(solution)/shard_map/all_to_all | solution.py:71
  26.4 12.4 %all-to-all-done = f32[32,1,3072]{2,1,0:T(1,128)S(1)} async-done(((f32[32,1,3072]{2,1,0:T(1,128)}), f32[32,1,3072]{2,1,0:T(1,128)S(1)}, u32[]{:S(2)}, u32[]{:S(2)}) %all-to-all-start) | async-done | bytes 393248 | tf_op jit(solution)/shard_map/all_to_all | solution.py:71
  48.0 3.3 collective-permute-done.1
  53.8 5.2 collective-permute-start.3
  60.5 51.6 %all-reduce.36 = (f32[1,16]{1,0:T(1,128)S(1)}, f32[1,16]{1,0:T(1,128)S(1)}) all-reduce(f32[1,16]{1,0:T(1,128)S(1)} %bitcast.84, f32[1,16]{1,0:T(1,128)S(1)} %bitcast.83), channel_id=1, replica_groups=mesh['subj'=32,'slab'=16] {'slab'}, use_global_device_ids=true, to_apply=%region_1.2 | all-reduce | flops 32 | bytes 256 | tf_op jit(solution)/shard_map/psum | solution.py:87
  112.4 42.8 %psum.114 = f32[1,16]{1,0:T(1,128)S(1)} all-reduce(f32[1,16]{1,0:T(1,128)S(1)} %bitcast.89), channel_id=1, replica_groups=mesh['subj'=32,'slab'=16] {'slab'}, use_global_device_ids=true, to_apply=%region_5.6 | all-reduce | flops 16 | bytes 128 | tf_op jit(solution)/shard_map/psum | solution.py:87
  157.6 2.5 collective-permute-start.5
  160.2 3.3 collective-permute-done.5
  164.7 48.8 %psum.115 = f32[1,16]{1,0:T(1,128)S(1)} all-reduce(f32[1,16]{1,0:T(1,128)S(1)} %bitcast.91), channel_id=1, replica_groups=mesh['subj'=32,'slab'=16] {'slab'}, use_global_device_ids=true, to_apply=%region_7.8 | all-reduce | flops 16 | bytes 128 | tf_op jit(solution)/shard_map/psum | solution.py:96
  215.0 42.8 %psum.116 = f32[1,16]{1,0:T(1,128)S(1)} all-reduce(f32[1,16]{1,0:T(1,128)S(1)} %bitcast.81), channel_id=1, replica_groups=mesh['subj'=32,'slab'=16] {'slab'}, use_global_device_ids=true, to_apply=%region_9.10 | all-reduce | flops 16 | bytes 128 | tf_op jit(solution)/shard_map/psum | solution.py:87
  260.7 2.5 collective-permute-start.7
  263.4 3.3 collective-permute-done.7
  267.8 48.8 %psum.117 = f32[1,16]{1,0:T(1,128)S(1)} all-reduce(f32[1,16]{1,0:T(1,128)S(1)} %bitcast.92), channel_id=1, replica_groups=mesh['subj'=32,'slab'=16] {'slab'}, use_global_device_ids=true, to_apply=%region_11.12 | all-reduce | flops 16 | bytes 128 | tf_op jit(solution)/shard_map/psum | solution.py:96
  317.5 42.8 %psum.118 = f32[1,16]{1,0:T(1,128)S(1)} all-reduce(f32[1,16]{1,0:T(1,128)S(1)} %bitcast.85), channel_id=1, replica_groups=mesh['subj'=32,'slab'=16] {'slab'}, use_global_device_ids=true, to_apply=%region_13.14 | all-reduce | flops 16 | bytes 128 | tf_op jit(solution)/shard_map/psum | solution.py:87
  365.9 3.3 collective-permute-done.9
  370.3 48.8 %psum.119 = f32[1,16]{1,0:T(1,128)S(1)} all-reduce(f32[1,16]{1,0:T(1,128)S(1)} %bitcast.93), channel_id=1, replica_groups=mesh['subj'=32,'slab'=16] {'slab'}, use_global_device_ids=true, to_apply=%region_15.16 | all-reduce | flops 16 | bytes 128 | tf_op jit(solution)/shard_map/psum | solution.py:96
  420.0 42.8 %psum.120 = f32[1,16]{1,0:T(1,128)S(1)} all-reduce(f32[1,16]{1,0:T(1,128)S(1)} %bitcast.86), channel_id=1, replica_groups=mesh['subj'=32,'slab'=16] {'slab'}, use_global_device_ids=true, to_apply=%region_17.18 | all-reduce | flops 16 | bytes 128 | tf_op jit(solution)/shard_map/psum | solution.py:87
  465.7 2.7 collective-permute-start.11
  468.6 3.1 collective-permute-done.11
  472.9 48.8 %psum.121 = f32[1,16]{1,0:T(1,128)S(1)} all-reduce(f32[1,16]{1,0:T(1,128)S(1)} %bitcast.94), channel_id=1, replica_groups=mesh['subj'=32,'slab'=16] {'slab'}, use_global_device_ids=true, to_apply=%region_19.20 | all-reduce | flops 16 | bytes 128 | tf_op jit(solution)/shard_map/psum | solution.py:96
  522.6 42.8 %psum.122 = f32[1,16]{1,0:T(1,128)S(1)} all-reduce(f32[1,16]{1,0:T(1,128)S(1)} %bitcast.87), channel_id=1, replica_groups=mesh['subj'=32,'slab'=16] {'slab'}, use_global_device_ids=true, to_apply=%region_21.22 | all-reduce | flops 16 | bytes 128 | tf_op jit(solution)/shard_map/psum | solution.py:87
  571.0 3.3 collective-permute-done.13
  575.4 48.8 %psum.123 = f32[1,16]{1,0:T(1,128)S(1)} all-reduce(f32[1,16]{1,0:T(1,128)S(1)} %bitcast.95), channel_id=1, replica_groups=mesh['subj'=32,'slab'=16] {'slab'}, use_global_device_ids=true, to_apply=%region_23.24 | all-reduce | flops 16 | bytes 128 | tf_op jit(solution)/shard_map/psum | solution.py:96
  625.7 42.9 %psum.124 = f32[1,16]{1,0:T(1,128)S(1)} all-reduce(f32[1,16]{1,0:T(1,128)} %bitcast.88), channel_id=1, replica_groups=mesh['subj'=32,'slab'=16] {'slab'}, use_global_device_ids=true, to_apply=%region_25.26 | all-reduce | flops 16 | bytes 128 | tf_op jit(solution)/shard_map/psum | solution.py:87
  674.2 3.3 collective-permute-done.15
  679.3 49.4 %psum.125 = f32[1,16]{1,0:T(1,128)} all-reduce(f32[1,16]{1,0:T(1,128)} %bitcast.96), channel_id=1, replica_groups=mesh['subj'=32,'slab'=16] {'slab'}, use_global_device_ids=true, to_apply=%region_27.28 | all-reduce | flops 16 | bytes 128 | tf_op jit(solution)/shard_map/psum | solution.py:96
  730.7 43.4 %psum.126 = f32[1,16]{1,0:T(1,128)} all-reduce(f32[1,16]{1,0:T(1,128)} %bitcast.90), channel_id=1, replica_groups=mesh['subj'=32,'slab'=16] {'slab'}, use_global_device_ids=true, to_apply=%region_29.30 | all-reduce | flops 16 | bytes 128 | tf_op jit(solution)/shard_map/psum | solution.py:87
  780.7 3.3 collective-permute-done.17
  785.8 48.9 %psum.127 = f32[1,16]{1,0:T(1,128)S(1)} all-reduce(f32[1,16]{1,0:T(1,128)} %bitcast.82), channel_id=1, replica_groups=mesh['subj'=32,'slab'=16] {'slab'}, use_global_device_ids=true, to_apply=%region_31.32 | all-reduce | flops 16 | bytes 128 | tf_op jit(solution)/shard_map/psum | solution.py:96
  836.4 8.3 copy.16
  844.7 9.8 reshape.129
  855.6 163.3 %reduce-scatter.4.cloned.1.call-done = f32[48,64]{1,0:T(8,128)} async-done(((f32[1536,64]{1,0:T(8,128)}), f32[48,64]{1,0:T(8,128)}) %reduce-scatter.4.cloned.1.call-update) | async-done | bytes 12304
  (153 shorter events, 72.4 us)
Async XLA Ops:
  7.2 44.2 %copy-start.7 = (f32[16]{0:T(128)S(1)}, f32[16]{0:T(128)}, u32[]{:S(2)}) copy-start(f32[16]{0:T(128)} %param.17) | copy-start | bytes 196
  7.2 44.1 %copy-start.5 = (f32[1,16,4,1536]{3,2,1,0:T(4,128)S(1)}, f32[1,16,4,1536]{3,2,1,0:T(4,128)}, u32[]{:S(2)}) copy-start(f32[1,16,4,1536]{3,2,1,0:T(4,128)} %param.10) | copy-start | bytes 1179652
  7.2 52.8 %copy-start.9 = (f32[1,16]{1,0:T(1,128)S(1)}, f32[1,16]{1,0:T(1,128)}, u32[]{:S(2)}) copy-start(f32[1,16]{1,0:T(1,128)} %param.12) | copy-start | bytes 196
  10.2 28.6 %all-to-all-start = ((f32[32,1,3072]{2,1,0:T(1,128)}), f32[32,1,3072]{2,1,0:T(1,128)S(1)}, u32[]{:S(2)}, u32[]{:S(2)}) async-start(f32[32,1,3072]{2,1,0:T(1,128)} %reshape.131), calls=%async_computation | async-start | bytes 786432 | tf_op jit(solution)/shard_map/all_to_all | solution.py:71
  23.9 995.0 %reduce-scatter.4.cloned.1.call-start = ((), (), s32[]{:S(2)}) async-start(), calls=%async_computation.2 | async-start | bytes 811008
  24.7 549.5 %copy-start.1 = (f32[4,1536]{1,0:T(4,128)}, f32[4,1536]{1,0:T(4,128)S(1)}, u32[]{:S(2)}) copy-start(f32[4,1536]{1,0:T(4,128)S(1)} %get-tuple-element.85) | copy-start | bytes 73732
  24.7 549.5 %copy-start.3 = (f32[4,1536]{1,0:T(4,128)}, f32[4,1536]{1,0:T(4,128)S(1)}, u32[]{:S(2)}) copy-start(f32[4,1536]{1,0:T(4,128)S(1)} %get-tuple-element.87) | copy-start | bytes 73732
  24.7 600.2 %copy-start.2 = (f32[4,1536]{1,0:T(4,128)}, f32[4,1536]{1,0:T(4,128)S(1)}, u32[]{:S(2)}) copy-start(f32[4,1536]{1,0:T(4,128)S(1)} %get-tuple-element.86) | copy-start | bytes 73732
  25.6 129.9 %copy-start.6 = (f32[16]{0:T(128)}, f32[16]{0:T(128)S(1)}, u32[]{:S(2)}) copy-start(f32[16]{0:T(128)S(1)} %get-tuple-element.90) | copy-start | bytes 196
  26.4 547.9 %copy-start.4 = (f32[4,1536]{1,0:T(4,128)}, f32[4,1536]{1,0:T(4,128)S(1)}, u32[]{:S(2)}) copy-start(f32[4,1536]{1,0:T(4,128)S(1)} %fusion.40) | copy-start | bytes 73732
  43.4 4.5 collective-permute-start
  45.4 5.9 collective-permute-start.1
  51.9 7.4 collective-permute-start.2
  53.8 6.2 collective-permute-start.3
  155.7 4.6 collective-permute-start.4
  157.6 5.9 collective-permute-start.5
  214.1 44.6 %copy-start.12 = (f32[16]{0:T(128)}, f32[16]{0:T(128)S(1)}, u32[]{:S(2)}) copy-start(f32[16]{0:T(128)S(1)} %divide_bitcast_fusion.12) | copy-start | bytes 196
  258.8 4.6 collective-permute-start.6
  260.7 5.9 collective-permute-start.7
  361.3 4.6 collective-permute-start.8
  363.2 5.9 collective-permute-start.9
  463.8 4.8 collective-permute-start.10
  465.7 5.9 collective-permute-start.11
  522.3 51.9 %copy-start.15 = (f32[16]{0:T(128)}, f32[16]{0:T(128)S(1)}, u32[]{:S(2)}) copy-start(f32[16]{0:T(128)S(1)} %divide_bitcast_fusion.6) | copy-start | bytes 196
  566.4 4.6 collective-permute-start.12
  568.3 5.9 collective-permute-start.13
  669.6 4.6 collective-permute-start.14
  671.5 5.9 collective-permute-start.15
  679.3 94.9 %copy-start = (f32[1,16,4,1536]{3,1,2,0:T(8,128)}, f32[1,16,4,1536]{3,1,2,0:T(8,128)S(1)}, u32[]{:S(2)}) copy-start(f32[1,16,4,1536]{3,1,2,0:T(8,128)S(1)} %get-tuple-element.9) | copy-start | bytes 1179652
  776.1 4.6 collective-permute-start.16
  778.0 5.9 collective-permute-start.17
  836.4 183.7 %copy-start.8 = (f32[16,4,48]{2,1,0:T(4,128)S(1)}, f32[16,4,48]{2,1,0:T(4,128)}, u32[]{:S(2)}) copy-start(f32[16,4,48]{2,1,0:T(4,128)} %param.19) | copy-start | bytes 36868
  (11 other events, 145.7 us)
Sparse Core Ops, SparseCore 0:
  854.7 164.1 reduce-scatter.3
